TPU v7x, 32 devices: a whole 2x2x4 slice. The times are simulated.
32 devices in a mesh: dp: 16 (over z, y, core), node: 2 (over x).
Axes of the slice: x: 2, y: 2, z: 4, core: 2. Of those that a mesh axis runs over, the one named last changes fastest.
Arguments:
- node_feats: bfloat16 [768, 25, 128], P(('dp', 'node')), may hold values from -2 to 2
- cotangent: bfloat16 [768, 25, 128], P(('dp', 'node')), may hold values from -3 to 3
- wigner: bfloat16 [13, 25, 8192], P(None, None, ('dp', 'node')), may hold values from -1.25 to 1.25
- radial: bfloat16 [2, 8192, 128], P(None, ('dp', 'node')), may hold values from 0.29882812 to 3
- edge_src: int32 [8192], P(('dp', 'node')), may hold values from 0 to 23
- edge_dst: int32 [8192], P(('dp', 'node')), may hold values from 0 to 23
- edge_count: int32 [32], P(('dp', 'node')), may hold values from 128 to 256
- params: float32 [2, 933888], P(None, ('dp', 'node')), may hold values from -0.5 to 0.5
- moment1: float32 [2, 933888], P(None, ('dp', 'node')), may hold values from -3 to 3
- moment2: float32 [2, 933888], P(None, ('dp', 'node')), may hold values from 1 to 100
Outputs:
- new_params: float32 [2, 933888], P(None, ('dp', 'node'))
- new_moment1: float32 [2, 933888], P(None, ('dp', 'node'))
- new_moment2: float32 [2, 933888], P(None, ('dp', 'node'))
Inputs may be any that keep to these rules, and one draw needn't show every extreme that they name: `edge_src`: atom numbers within the edge's own structure. `edge_dst`: atom numbers within the edge's own structure. `edge_count`: slots from this number on within a structure are padding.
All inputs are finite; a program needn't handle non-finite values.
Results may differ from a plain program's by a relative error of at most 0.017.
Values may be sent and summed in bfloat16 or wider, within the bound.
A program may use at most 64 MiB of HBM per device.

v0:
```python
import functools

import jax
import jax.numpy as jnp
from jax import lax
from jax.experimental import pallas as pl
from jax.experimental.pallas import tpu as pltpu
from jax.sharding import PartitionSpec as P

AVG = 10
LANES = 128
PIECES = 3
LINK = jnp.bfloat16


def split_axes(mesh):
    rest = mesh.shape["dp"] // 2
    y = 1
    while y * y * 4 <= rest and rest % (y * 2) == 0:
        y *= 2
    return rest // y, y, mesh.shape["node"]


def place(dims):
    zs, ys, xs = dims
    dp = lax.axis_index("dp")
    x = lax.axis_index("node")
    core = lax.rem(dp, 2)
    y = lax.rem(dp // 2, ys)
    z = dp // (2 * ys)
    return {"z": z, "y": y, "c": core, "x": x}


def device(dims, at):
    return {"dp": (at["z"] * dims[1] + at["y"]) * 2 + at["c"], "node": at["x"]}


def peer_of(dims, me, axis, step):
    size = {"z": dims[0], "y": dims[1], "c": 2, "x": dims[2]}[axis]
    other = dict(me)
    other[axis] = lax.rem(me[axis] + step, size)
    return other


def size_of(dims, axis):
    return {"z": dims[0], "y": dims[1], "c": 2, "x": dims[2]}[axis]


def greet(dims, me):
    barrier = pltpu.get_barrier_semaphore()
    count = 0
    for axis in "zyxc":
        for step in range(1, size_of(dims, axis)):
            pl.semaphore_signal(
                barrier,
                inc=1,
                device_id=device(dims, peer_of(dims, me, axis, step)),
                device_id_type=pl.DeviceIdType.MESH,
            )
            count += 1
    pl.semaphore_wait(barrier, count)


def gather_kernel(dims, own_ref, out_ref, local_sem, send_sem, recv_sem):
    me = place(dims)
    layers, rows = own_ref.shape[0], own_ref.shape[1]
    part = rows // PIECES
    greet(dims, me)
    mine = pltpu.make_async_copy(
        own_ref, out_ref.at[:, me["z"], me["y"], me["c"], me["x"]], local_sem
    )
    mine.start()

    def view(ref, layer, piece, spans, at):
        index = [layer]
        for axis in "zycx":
            index.append(slice(None) if axis in spans else at[axis])
        index.append(pl.ds(piece * part, part))
        return ref.at[tuple(index)]

    items = []
    for layer in range(layers):
        for piece in range(PIECES):
            order = "zyxc" if (layer * PIECES + piece) % 2 == 0 else "zxyc"
            items.append((layer, piece, order))
    most = max(size_of(dims, a) for a in "zyxc") - 1
    started = []
    for phase in range(4):
        for number, (layer, piece, order) in enumerate(items):
            spans = order[:phase]
            if phase:
                for copy in started[(phase - 1) * len(items) + number]:
                    copy.wait_recv()
            axis = order[phase]
            copies = []
            for step in range(1, size_of(dims, axis)):
                if phase == 0:
                    src = own_ref.at[layer, pl.ds(piece * part, part)]
                else:
                    src = view(out_ref, layer, piece, spans, me)
                slot = (number * 4 + phase) * most + step - 1
                copy = pltpu.make_async_remote_copy(
                    src_ref=src,
                    dst_ref=view(out_ref, layer, piece, spans, me),
                    send_sem=send_sem.at[slot],
                    recv_sem=recv_sem.at[slot],
                    device_id=device(dims, peer_of(dims, me, axis, step)),
                    device_id_type=pl.DeviceIdType.MESH,
                )
                copy.start()
                copies.append(copy)
            started.append(copies)
        if phase == 0:
            mine.wait()
    for copies in started[3 * len(items) :]:
        for copy in copies:
            copy.wait_recv()
    for copies in started:
        for copy in copies:
            copy.wait_send()


def gather_shards(dims, own, collective_id):
    layers, rows, lanes = own.shape
    zs, ys, xs = dims
    most = max(zs, ys, xs, 2) - 1
    slots = layers * PIECES * 4 * most
    return pl.pallas_call(
        functools.partial(gather_kernel, dims),
        out_shape=jax.ShapeDtypeStruct((layers, zs, ys, 2, xs, rows, lanes), own.dtype),
        in_specs=[pl.BlockSpec(memory_space=pltpu.VMEM)],
        out_specs=pl.BlockSpec(memory_space=pltpu.VMEM),
        scratch_shapes=[
            pltpu.SemaphoreType.DMA,
            pltpu.SemaphoreType.DMA((slots,)),
            pltpu.SemaphoreType.DMA((slots,)),
        ],
        compiler_params=pltpu.CompilerParams(
            collective_id=collective_id, has_side_effects=True, vmem_limit_bytes=48 << 20
        ),
        name="gather_shards",
    )(own)


def reduce_buffers(dims, pairs, part):
    zs = dims[0]
    buffers = []
    for first, second, count in pairs:
        n1, n2 = size_of(dims, first), size_of(dims, second)
        buffers += [
            pltpu.VMEM((count, zs, n2, part, LANES), jnp.float32),
            pltpu.VMEM((count, n1 - 1, zs, n2, part, LANES), LINK),
            pltpu.VMEM((count, n1 - 1, zs, n2, part, LANES), LINK),
            pltpu.VMEM((count, zs, part, LANES), jnp.float32),
            pltpu.VMEM((count, n2 - 1, zs, part, LANES), LINK),
            pltpu.VMEM((count, n2 - 1, zs, part, LANES), LINK),
            pltpu.VMEM((count, part, LANES), jnp.float32),
            pltpu.VMEM((count, zs - 1, part, LANES), LINK),
            pltpu.VMEM((count, zs - 1, part, LANES), LINK),
        ]
    return buffers


def reduce_items(layers):
    items = []
    for layer in reversed(range(layers)):
        for piece in range(PIECES):
            number = len(items)
            items.append((layer, piece, number % 2, number // 2))
    return items


def reduce_kernel(dims, grad_ref, out_ref, pair_buf, *scratch):
    zs = dims[0]
    buffers = (scratch[:9], scratch[9:18])
    send_sem, recv_sem = scratch[18:]
    me = place(dims)
    layers, rows = out_ref.shape[0], out_ref.shape[1]
    part = rows // PIECES
    greet(dims, me)
    items = reduce_items(layers)
    most = max(size_of(dims, a) for a in "zyxc") - 1
    pending = []

    def send(number, phase, step, axis, src, dst):
        slot = (number * 4 + phase) * most + step - 1
        copy = pltpu.make_async_remote_copy(
            src_ref=src,
            dst_ref=dst,
            send_sem=send_sem.at[slot],
            recv_sem=recv_sem.at[slot],
            device_id=device(dims, peer_of(dims, me, axis, step)),
            device_id_type=pl.DeviceIdType.MESH,
        )
        copy.start()
        pending.append(copy)
        return copy

    def f32(value):
        return value.astype(jnp.float32)

    waits = {}
    for number, (layer, piece, kind, place_in) in enumerate(items):
        span = pl.ds(piece * part, part)
        waits[number] = [
            send(
                number, 0, 1, "c",
                grad_ref.at[layer, :, :, 1 - me["c"], :, span], pair_buf.at[number],
            )
        ]
    for phase in range(4):
        for number, (layer, piece, kind, place_in) in enumerate(items):
            span = pl.ds(piece * part, part)
            acc1, send1, recv1, acc2, send2, recv2, acc3, send3, recv3 = (
                buf.at[place_in] for buf in buffers[kind]
            )
            first, second = ("x", "y") if kind == 0 else ("y", "x")
            n1, n2 = size_of(dims, first), size_of(dims, second)
            for copy in waits[number]:
                copy.wait_recv()
            copies = []
            if phase == 0:
                for step in list(range(1, n1)) + [0]:
                    k1 = lax.rem(me[first] + step, n1)

                    def one(i, carry, step=step, k1=k1):
                        z, k2 = i // n2, lax.rem(i, n2)
                        y, x = (k2, k1) if kind == 0 else (k1, k2)
                        total = f32(grad_ref[layer, z, y, me["c"], x, span]) + f32(
                            pair_buf[number, z, y, x]
                        )
                        if step:
                            send1[step - 1, z, k2] = total.astype(LINK)
                        else:
                            acc1[z, k2] = total
                        return carry

                    lax.fori_loop(0, zs * n2, one, 0)
                    if step:
                        copies.append(
                            send(number, 1, step, first, send1.at[step - 1], recv1.at[step - 1])
                        )
            elif phase == 1:
                for step in list(range(1, n2)) + [0]:
                    k2 = lax.rem(me[second] + step, n2)

                    def one(z, carry, step=step, k2=k2):
                        total = acc1[z, k2]
                        for e in range(n1 - 1):
                            total = total + f32(recv1[e, z, k2])
                        if step:
                            send2[step - 1, z] = total.astype(LINK)
                        else:
                            acc2[z] = total
                        return carry

                    lax.fori_loop(0, zs, one, 0)
                    if step:
                        copies.append(
                            send(number, 2, step, second, send2.at[step - 1], recv2.at[step - 1])
                        )
            elif phase == 2:
                for step in list(range(1, zs)) + [0]:
                    z = lax.rem(me["z"] + step, zs)
                    total = acc2[z]
                    for e in range(n2 - 1):
                        total = total + f32(recv2[e, z])
                    if step:
                        send3[step - 1] = total.astype(LINK)
                        copies.append(
                            send(number, 3, step, "z", send3.at[step - 1], recv3.at[step - 1])
                        )
                    else:
                        acc3[...] = total
            else:
                total = acc3[...]
                for e in range(zs - 1):
                    total = total + f32(recv3[e])
                out_ref[layer, span] = total
            waits[number] = copies
    for copy in pending:
        copy.wait_send()


def reduce_shards(dims, grad, collective_id):
    layers, zs, ys, _, xs, rows, lanes = grad.shape
    part = rows // PIECES
    most = max(zs, ys, xs, 2) - 1
    count = layers * PIECES
    slots = count * 4 * most
    even, odd = (count + 1) // 2, count // 2
    return pl.pallas_call(
        functools.partial(reduce_kernel, dims),
        out_shape=jax.ShapeDtypeStruct((layers, rows, lanes), jnp.float32),
        in_specs=[pl.BlockSpec(memory_space=pltpu.VMEM)],
        out_specs=pl.BlockSpec(memory_space=pltpu.VMEM),
        scratch_shapes=[pltpu.VMEM((count, zs, ys, xs, part, lanes), grad.dtype)]
        + reduce_buffers(dims, (("x", "y", even), ("y", "x", odd)), part)
        + [pltpu.SemaphoreType.DMA((slots,)), pltpu.SemaphoreType.DMA((slots,))],
        compiler_params=pltpu.CompilerParams(
            collective_id=collective_id, has_side_effects=True, vmem_limit_bytes=48 << 20
        ),
        name="reduce_shards",
    )(grad)


def layer(x, weights, wig, rad, gather, scatter):
    nat, coef, chan = x.shape
    wzero, wreal, wimag = weights
    rows = wig.shape[1]
    lone = (rows + 2) // 3
    lmore = lone - 1
    edges = gather.shape[0]
    kzero, kone = lone * chan, lmore * chan
    xs = jnp.dot(gather, x.reshape(nat, coef * chan), preferred_element_type=jnp.float32)
    xs = xs.astype(jnp.bfloat16).reshape(edges, coef, chan)
    rot = jnp.einsum("ekj,ejc->ekc", wig, xs, preferred_element_type=jnp.float32)
    rot = (rot * rad.astype(jnp.float32)[:, None, :]).astype(jnp.bfloat16)
    azero = rot[:, :lone].reshape(edges, kzero)
    aplus = rot[:, lone : lone + lmore].reshape(edges, kone)
    aminus = rot[:, lone + lmore :].reshape(edges, kone)
    dot = functools.partial(jnp.dot, preferred_element_type=jnp.float32)
    yzero = dot(azero, wzero)
    yplus = dot(aplus, wreal) - dot(aminus, wimag)
    yminus = dot(aplus, wimag) + dot(aminus, wreal)
    mixed = jnp.concatenate([yzero, yplus, yminus], axis=1).astype(jnp.bfloat16)
    mixed = mixed.reshape(edges, rows, chan)
    message = jnp.einsum("ekj,ekc->ejc", wig, mixed, preferred_element_type=jnp.float32)
    summed = jnp.dot(scatter, message.reshape(edges, coef * chan), precision=lax.Precision.HIGH)
    aggregated = summed.reshape(nat, coef, chan) / AVG
    out = x.astype(jnp.float32) + aggregated
    scalar = out[:, 0, :]
    gated = jnp.concatenate(
        [jax.nn.silu(scalar)[:, None, :], out[:, 1:, :] * jax.nn.sigmoid(scalar)[:, None, :]],
        axis=1,
    )
    return gated.astype(jnp.bfloat16)


def local(
    dims, node_feats, cotangent, wigner, radial, edge_src, edge_dst, edge_count, params, moment1,
    moment2,
):
    nat, coef, chan = node_feats.shape
    layers, length = params.shape
    zs, ys, xs = dims
    shards = zs * ys * 2 * xs
    block = LANES * 16 * PIECES
    padded = -(-length // block) * block
    rows = padded // LANES
    own = jnp.pad(params.astype(jnp.bfloat16), ((0, 0), (0, padded - length)))
    full = gather_shards(dims, own.reshape(layers, rows, LANES), 0)
    full = full.reshape(layers, shards, rows, LANES)
    if length % LANES == 0:
        full = full[:, :, : length // LANES]
    else:
        full = full.reshape(layers, shards, padded)[:, :, :length]
    full = full.reshape(layers, shards * length // LANES, LANES)
    lone = (wigner.shape[0] + 2) // 3
    kzero, kone = lone * chan, (lone - 1) * chan
    cut = kzero * kzero // LANES
    step = kone * kone // LANES

    def unpack(flat):
        return (
            flat[:cut].reshape(kzero, kzero),
            flat[cut : cut + step].reshape(kone, kone),
            flat[cut + step :].reshape(kone, kone),
        )

    def pack(grads):
        return jnp.concatenate([g.reshape(-1, LANES) for g in grads], axis=0)

    edges = edge_src.shape[0]
    atoms = jnp.arange(nat, dtype=jnp.int32)
    valid = jnp.arange(edges, dtype=jnp.int32) < edge_count[0]
    gather = (edge_src[:, None] == atoms[None, :]).astype(jnp.bfloat16)
    scatter = jnp.where(valid[None, :], edge_dst[None, :] == atoms[:, None], False)
    scatter = scatter.astype(jnp.float32)
    wig = jnp.transpose(wigner, (2, 0, 1))

    def first(wts):
        return layer(node_feats, wts, wig, radial[0], gather, scatter)

    def second(hidden, wts):
        return layer(hidden, wts, wig, radial[1], gather, scatter)

    hidden, pull_first = jax.vjp(first, unpack(full[0]))
    _, pull_second = jax.vjp(second, hidden, unpack(full[1]))
    back, grad_second = pull_second(cotangent)
    (grad_first,) = pull_first(back)
    grad = jnp.stack([pack(grad_first), pack(grad_second)])
    if length % LANES == 0:
        grad = grad.reshape(layers, shards, length // LANES, LANES)
        grad = jnp.pad(grad, ((0, 0), (0, 0), (0, rows - length // LANES), (0, 0)))
    else:
        grad = grad.reshape(layers, shards, length)
        grad = jnp.pad(grad, ((0, 0), (0, 0), (0, padded - length)))
    owned = reduce_shards(dims, grad.reshape(layers, zs, ys, 2, xs, rows, LANES), 1)
    grad = owned.reshape(layers, padded)[:, :length]
    new_moment1 = 0.9 * moment1 + 0.1 * grad
    new_moment2 = 0.95 * moment2 + 0.05 * grad * grad
    m_hat = new_moment1 / (1.0 - 0.9**60)
    v_hat = new_moment2 / (1.0 - 0.95**60)
    new_params = params - 0.01 * (m_hat / (jnp.sqrt(v_hat) + 1e-08) + 0.1 * params)
    return (new_params, new_moment1, new_moment2)


def solution(mesh):
    both = ("dp", "node")
    return jax.shard_map(
        functools.partial(local, split_axes(mesh)),
        mesh=mesh,
        in_specs=(
            P(both, None, None),
            P(both, None, None),
            P(None, None, both),
            P(None, both, None),
            P(both),
            P(both),
            P(both),
            P(None, both),
            P(None, both),
            P(None, both),
        ),
        out_specs=(P(None, both), P(None, both), P(None, both)),
        check_vma=False,
    )
```

profile of v0, /device:TPU:0, one launch (start us, length us, event | category | flops | bytes accessed | tf_op | source)
XLA Modules:
  0.0 205.2 jit_solution(15205792109618804632)
XLA Ops:
  5.7 2.3 %copy.23 = bf16[256,3200]{0,1:T(8,128)(2,1)} copy(bf16[256,3200]{1,0:T(8,128)(2,1)S(1)} %convolution_convert_fusion.1) | data formatting | bytes 3276800 | tf_op jit(solution)/shard_map/jvp()/convert_element_type | solution.py:316
  8.0 3.4 %copy.24 = bf16[256,25,128]{2,1,0:T(8,128)(2,1)S(1)} copy(bf16[256,25,128]{0,2,1:T(8,128)(2,1)} %bitcast.224) | data formatting | bytes 3276800 | tf_op jit(solution)/shard_map/jvp()/reshape | solution.py:316
  13.4 33.8 %gather_shards.1 = bf16[2,4,2,2,2,240,128]{6,5,4,3,2,1,0:T(8,128)(2,1)S(1)} custom-call(bf16[2,240,128]{2,1,0:T(8,128)(2,1)S(1)} %bitcast.213), custom_call_target="tpu_custom_call" | custom-call | tf_op jit(solution)/shard_map/gather_shards/pallas_call | solution.py:128
  61.7 2.8 %convolution_bitcast_fusion.1 = f32[256,25,128]{2,1,0:T(8,128)} fusion(bf16[256,13,128]{2,1,0:T(8,128)(2,1)S(1)} %copy.28, bf16[256,13,25]{2,1,0:T(8,128)(2,1)S(1)} %copy.25), kind=kOutput, calls=%fused_computation.16 | convolution fusion | flops 21299200 | bytes 4295168 | tf_op jit(solution)/shard_map/jvp(ekj,ekc->ejc)/dot_general | solution.py:328
  64.5 5.0 %copy.30 = f32[256,25,128]{0,2,1:T(8,128)} copy(f32[256,25,128]{2,1,0:T(8,128)} %convolution_bitcast_fusion.1) | data formatting | bytes 6553600 | tf_op jit(solution)/shard_map/jvp(ekj,ekc->ejc)/dot_general | solution.py:328
  70.1 2.9 %fusion.36 = f32[24,25,128]{2,0,1:T(8,128)S(1)} fusion(f32[256,25,128]{0,2,1:T(8,128)} %copy.30, bf16[24,25,128]{2,0,1:T(8,128)(2,1)S(1)} %copy-done.25, s32[256]{0:T(256)S(1)} %copy-done.33, pred[256]{0:T(512)(128)(4,1)S(1)} %iota_compare_fusion.5), kind=kOutput, calls=%fused_computation.59 | convolution fusion | flops 118207488 | bytes 3738880 | tf_op jit(solution)/shard_map/jvp()/dot_general | solution.py:329
  74.4 2.3 %copy.32 = bf16[256,3200]{0,1:T(8,128)(2,1)} copy(bf16[256,3200]{1,0:T(8,128)(2,1)S(1)} %convolution_convert_fusion) | data formatting | bytes 3276800 | tf_op jit(solution)/shard_map/jvp()/convert_element_type | solution.py:316
  76.7 3.4 %copy.33 = bf16[256,25,128]{2,1,0:T(8,128)(2,1)S(1)} copy(bf16[256,25,128]{0,2,1:T(8,128)(2,1)} %bitcast.225) | data formatting | bytes 3276800 | tf_op jit(solution)/shard_map/jvp()/reshape | solution.py:316
  90.0 2.4 %fusion.136 = (bf16[256,4,128]{2,1,0:T(4,128)(2,1)S(1)}, bf16[256,4,128]{2,1,0:T(4,128)(2,1)}) fusion(bf16[256,13,128]{2,1,0:T(8,128)(2,1)} %copy-done.7), kind=kLoop, calls=%fused_computation.179 | loop fusion | bytes 1048576 | tf_op jit(solution)/shard_map/jvp()/slice | solution.py:320
  100.8 2.6 %copy.37 = bf16[256,13,128]{2,1,0:T(8,128)(2,1)} copy(bf16[256,13,128]{0,2,1:T(8,128)(2,1)} %bitcast.249) | data formatting | bytes 1703936 | tf_op jit(solution)/shard_map/jvp()/convert_element_type | solution.py:326
  103.4 4.0 %convolution_bitcast_fusion = f32[256,25,128]{2,1,0:T(8,128)} fusion(bf16[256,13,128]{2,1,0:T(8,128)(2,1)} %copy.37, bf16[256,13,25]{2,1,0:T(8,128)(2,1)S(1)} %copy.25), kind=kOutput, calls=%fused_computation.15 | convolution fusion | flops 21299200 | bytes 4295168 | tf_op jit(solution)/shard_map/jvp(ekj,ekc->ejc)/dot_general | solution.py:328
  107.4 4.9 %copy.39 = f32[256,25,128]{0,2,1:T(8,128)} copy(f32[256,25,128]{2,1,0:T(8,128)} %convolution_bitcast_fusion) | data formatting | bytes 6553600 | tf_op jit(solution)/shard_map/jvp(ekj,ekc->ejc)/dot_general | solution.py:328
  112.4 2.9 %fusion.42 = f32[24,25,128]{2,0,1:T(8,128)S(1)} fusion(f32[256,25,128]{0,2,1:T(8,128)} %copy.39, bf16[24,24,128]{2,0,1:T(8,128)(2,1)S(1)} %slice_multiply_fusion.2, bf16[24,1,128]{2,0,1:T(8,128)(2,1)S(1)} %copy-done.32, s32[256]{0:T(256)S(1)} %copy-done.34, pred[256]{0:T(512)(128)(4,1)S(1)} %copy-done.39), kind=kOutput, calls=%fused_computation.61 | convolution fusion | flops 118284288 | bytes 3738880 | tf_op jit(solution)/shard_map/jvp()/dot_general | solution.py:329
  116.6 2.1 %fusion.20 = bf16[256,13,128]{2,1,0:T(8,128)(2,1)} fusion(bf16[256,13,25]{2,1,0:T(8,128)(2,1)S(1)} %copy.25, bf16[256,25,128]{2,0,1:T(8,128)(2,1)S(1)} %fusion.54), kind=kOutput, calls=%fused_computation.28 | convolution fusion | flops 21299200 | bytes 2656768 | tf_op jit(solution)/shard_map/transpose(jvp(ekj,ekc->ejc))/dot_general | solution.py:328
  129.3 2.6 %copy.47 = bf16[256,13,128]{2,1,0:T(8,128)(2,1)} copy(bf16[256,13,128]{0,2,1:T(8,128)(2,1)} %convert_multiply_fusion) | data formatting | bytes 1703936 | tf_op jit(solution)/shard_map/transpose(jvp())/mul | solution.py:318
  131.9 3.4 %convert_bitcast_fusion = bf16[256,25,128]{2,1,0:T(8,128)(2,1)} fusion(bf16[256,13,128]{2,1,0:T(8,128)(2,1)} %copy.47, bf16[256,13,25]{2,1,0:T(8,128)(2,1)S(1)} %copy.25), kind=kOutput, calls=%fused_computation.17 | convolution fusion | flops 21299200 | bytes 2656768 | tf_op jit(solution)/shard_map/transpose(jvp(ekj,ejc->ekc))/dot_general | solution.py:317
  135.3 4.2 %copy.49 = bf16[256,25,128]{0,2,1:T(8,128)(2,1)} copy(bf16[256,25,128]{2,1,0:T(8,128)(2,1)} %convert_bitcast_fusion) | data formatting | bytes 3276800 | tf_op jit(solution)/shard_map/transpose(jvp(ekj,ejc->ekc))/convert_element_type | solution.py:317
  139.5 2.1 %fusion.47 = bf16[3,25,8,128]{3,2,1,0:T(8,128)(2,1)S(1)} fusion(bf16[256,3200]{0,1:T(8,128)(2,1)} %bitcast.226, s32[256]{0:T(256)S(1)} %copy-done.37), kind=kOutput, calls=%fused_computation.64 | convolution fusion | flops 39410688 | bytes 1793024 | tf_op jit(solution)/shard_map/transpose(jvp())/dot_general | solution.py:315
  142.9 2.1 %fusion.17 = bf16[256,13,128]{2,1,0:T(8,128)(2,1)} fusion(bf16[256,13,25]{2,1,0:T(8,128)(2,1)S(1)} %copy.25, bf16[256,25,128]{2,0,1:T(8,128)(2,1)S(1)} %fusion.51), kind=kOutput, calls=%fused_computation.27 | convolution fusion | flops 21299200 | bytes 2656768 | tf_op jit(solution)/shard_map/transpose(jvp(ekj,ekc->ejc))/dot_general | solution.py:328
  148.3 2.4 %reshape.201 = bf16[3200,128]{1,0:T(8,128)(2,1)} reshape(bf16[640,640]{1,0:T(8,128)(2,1)} %convolution_convert_fusion.4) | data formatting | bytes 1638400 | tf_op jit(solution)/shard_map/reshape | solution.py:372
  154.6 2.5 %pad_maximum_fusion = bf16[7296,128]{1,0:T(8,128)(2,1)} fusion(bf16[2048,128]{1,0:T(8,128)(2,1)S(1)} %reshape.203, bf16[2048,128]{1,0:T(8,128)(2,1)S(1)} %reshape.202, bf16[3200,128]{1,0:T(8,128)(2,1)} %reshape.201), kind=kLoop, calls=%fused_computation.20 | loop fusion | flops 5603328 | bytes 3735552 | tf_op jit(solution)/shard_map/concatenate | solution.py:372
  157.1 3.7 %stack.9 = bf16[1,32,228,128]{3,2,1,0:T(8,128)(2,1)} reshape(bf16[7296,128]{1,0:T(8,128)(2,1)} %pad_maximum_fusion) | data formatting | bytes 3735552 | tf_op jit(solution)/shard_map/stack | solution.py:392
  165.3 3.8 %stack.10 = bf16[1,32,228,128]{3,2,1,0:T(8,128)(2,1)} reshape(bf16[7296,128]{1,0:T(8,128)(2,1)} %pad_maximum_fusion.1) | data formatting | bytes 3735552 | tf_op jit(solution)/shard_map/stack | solution.py:392
  170.8 32.6 %reduce_shards.1 = f32[2,240,128]{2,1,0:T(8,128)S(1)} custom-call(bf16[2,4,2,2,2,240,128]{6,5,4,3,2,1,0:T(8,128)(2,1)S(1)} %bitcast.210), custom_call_target="tpu_custom_call" | custom-call | tf_op jit(solution)/shard_map/reduce_shards/pallas_call | solution.py:292
  (171 shorter events, 68.9 us)
Async XLA Ops:
  64.5 5.6 %copy-start.25 = (bf16[24,25,128]{2,0,1:T(8,128)(2,1)S(1)}, bf16[24,25,128]{2,0,1:T(8,128)(2,1)}, u32[]{:S(2)}) copy-start(bf16[24,25,128]{2,0,1:T(8,128)(2,1)} %param.10) | copy-start | bytes 460804
  64.5 5.6 %copy-start.33 = (s32[256]{0:T(256)S(1)}, s32[256]{0:T(256)}, u32[]{:S(2)}) copy-start(s32[256]{0:T(256)} %param.15) | copy-start | bytes 3076
  70.1 3.0 %copy-start.38 = (pred[256]{0:T(512)(128)(4,1)}, pred[256]{0:T(512)(128)(4,1)S(1)}, u32[]{:S(2)}) copy-start(pred[256]{0:T(512)(128)(4,1)S(1)} %iota_compare_fusion.5) | copy-start | bytes 772
  70.1 3.7 %copy-start.36 = (s32[256]{0:T(256)S(1)}, s32[256]{0:T(256)}, u32[]{:S(2)}) copy-start(s32[256]{0:T(256)} %param.14) | copy-start | bytes 3076
  73.8 2.9 %copy-start.31 = (bf16[24,1,128]{2,0,1:T(8,128)(2,1)}, bf16[24,1,128]{2,0,1:T(8,128)(2,1)S(1)}, u32[]{:S(2)}) copy-start(bf16[24,1,128]{2,0,1:T(8,128)(2,1)S(1)} %slice_multiply_fusion.4) | copy-start | bytes 18436
  82.7 2.9 %copy-start = (bf16[1,32,228,128]{3,2,1,0:T(8,128)(2,1)S(1)}, bf16[1,32,228,128]{3,2,1,0:T(8,128)(2,1)}, u32[]{:S(2)}) copy-start(bf16[1,32,228,128]{3,2,1,0:T(8,128)(2,1)} %get-tuple-element.6) | copy-start | bytes 5603332
  88.7 4.7 %copy-start.3 = (bf16[640,640]{1,0:T(8,128)(2,1)}, bf16[640,640]{1,0:T(8,128)(2,1)S(1)}, u32[]{:S(2)}) copy-start(bf16[640,640]{1,0:T(8,128)(2,1)S(1)} %reshape.184) | copy-start | bytes 2457604
  88.8 3.6 %copy-start.2 = (bf16[7296,128]{1,0:T(8,128)(2,1)S(1)}, bf16[7296,128]{1,0:T(8,128)(2,1)}, u32[]{:S(2)}) copy-start(bf16[7296,128]{1,0:T(8,128)(2,1)} %squeeze.15) | copy-start | bytes 5603332
  92.4 6.4 %copy-start.4 = (bf16[256,4,128]{2,1,0:T(4,128)(2,1)}, bf16[256,4,128]{2,1,0:T(4,128)(2,1)S(1)}, u32[]{:S(2)}) copy-start(bf16[256,4,128]{2,1,0:T(4,128)(2,1)S(1)} %get-tuple-element.12) | copy-start | bytes 786436
  93.5 3.9 %copy-start.10 = (bf16[256,4,128]{2,1,0:T(4,128)(2,1)S(1)}, bf16[256,4,128]{2,1,0:T(4,128)(2,1)}, u32[]{:S(2)}) copy-start(bf16[256,4,128]{2,1,0:T(4,128)(2,1)} %get-tuple-element.13) | copy-start | bytes 786436
  107.4 5.0 %copy-start.32 = (bf16[24,1,128]{2,0,1:T(8,128)(2,1)S(1)}, bf16[24,1,128]{2,0,1:T(8,128)(2,1)}, u32[]{:S(2)}) copy-start(bf16[24,1,128]{2,0,1:T(8,128)(2,1)} %copy-done.31) | copy-start | bytes 18436
  107.4 5.0 %copy-start.34 = (s32[256]{0:T(256)S(1)}, s32[256]{0:T(256)}, u32[]{:S(2)}) copy-start(s32[256]{0:T(256)} %param.15) | copy-start | bytes 3076
  107.4 5.0 %copy-start.39 = (pred[256]{0:T(512)(128)(4,1)S(1)}, pred[256]{0:T(512)(128)(4,1)}, u32[]{:S(2)}) copy-start(pred[256]{0:T(512)(128)(4,1)} %copy-done.38) | copy-start | bytes 772
  112.4 3.0 %copy-start.28 = (bf16[24,25,128]{2,0,1:T(8,128)(2,1)S(1)}, bf16[24,25,128]{2,0,1:T(8,128)(2,1)}, u32[]{:S(2)}) copy-start(bf16[24,25,128]{2,0,1:T(8,128)(2,1)} %param.11) | copy-start | bytes 460804
  124.1 3.0 %copy-start.21 = (f32[256,128]{1,0:T(8,128)S(1)}, f32[256,128]{1,0:T(8,128)}, u32[]{:S(2)}) copy-start(f32[256,128]{1,0:T(8,128)} %get-tuple-element.20) | copy-start | bytes 393220
  124.5 2.8 %copy-start.22 = (bf16[256,512]{0,1:T(8,128)(2,1)S(1)}, bf16[256,512]{0,1:T(8,128)(2,1)}, u32[]{:S(2)}) copy-start(bf16[256,512]{0,1:T(8,128)(2,1)} %copy.58) | copy-start | bytes 786436
  135.3 4.2 %copy-start.37 = (s32[256]{0:T(256)S(1)}, s32[256]{0:T(256)}, u32[]{:S(2)}) copy-start(s32[256]{0:T(256)} %param.14) | copy-start | bytes 3076
  135.3 6.3 %copy-start.19 = (f32[24,24,128]{2,0,1:T(8,128)S(1)}, f32[24,24,128]{2,0,1:T(8,128)}, u32[]{:S(2)}) copy-start(f32[24,24,128]{2,0,1:T(8,128)} %copy-done.18) | copy-start | bytes 884740
  146.9 4.1 %copy-start.9 = (bf16[256,4,128]{2,1,0:T(4,128)(2,1)S(1)}, bf16[256,4,128]{2,1,0:T(4,128)(2,1)}, u32[]{:S(2)}) copy-start(bf16[256,4,128]{2,1,0:T(4,128)(2,1)} %get-tuple-element.14) | copy-start | bytes 786436
  157.1 3.7 %copy-start.15 = (bf16[256,5,128]{0,2,1:T(8,128)(2,1)S(1)}, bf16[256,5,128]{0,2,1:T(8,128)(2,1)}, u32[]{:S(2)}) copy-start(bf16[256,5,128]{0,2,1:T(8,128)(2,1)} %copy.35) | copy-start | bytes 983044
  165.3 3.8 %copy-start.1 = (bf16[1,32,228,128]{3,2,1,0:T(8,128)(2,1)S(1)}, bf16[1,32,228,128]{3,2,1,0:T(8,128)(2,1)}, u32[]{:S(2)}) copy-start(bf16[1,32,228,128]{3,2,1,0:T(8,128)(2,1)} %stack.9) | copy-start | bytes 5603332
  170.7 32.8 %copy-start.24 = (f32[2,29184]{1,0:T(2,128)S(1)}, f32[2,29184]{1,0:T(2,128)}, u32[]{:S(2)}) copy-start(f32[2,29184]{1,0:T(2,128)} %param.17) | copy-start | bytes 700420
  170.7 32.8 %copy-start.26 = (f32[2,29184]{1,0:T(2,128)S(1)}, f32[2,29184]{1,0:T(2,128)}, u32[]{:S(2)}) copy-start(f32[2,29184]{1,0:T(2,128)} %param.18) | copy-start | bytes 700420
  170.8 32.8 %copy-start.27 = (f32[2,29184]{1,0:T(2,128)S(1)}, f32[2,29184]{1,0:T(2,128)}, u32[]{:S(2)}) copy-start(f32[2,29184]{1,0:T(2,128)} %param.19) | copy-start | bytes 700420
  (20 other events, 31.3 us)
where the time goes:
time: 207 us; the launch traced here: 205 us
  local copies, waits for them, and re-layouts  78.9 us (38%)
  Pallas kernels  66.5 us (32%)
  matrix products  45.4 us (22%)
  other arithmetic  12.3 us (6%)
  between operations  2.16 us (1%)
    pallas_call x1, Pallas kernels, gather_shards(): pl.pallas_call(functools.partial(gather_kernel, dims), out_shape=jax.Shap...  33.8 us
    pallas_call x1, Pallas kernels, reduce_shards(): pl.pallas_call(functools.partial(reduce_kernel, dims), out_shape=jax.Shap...  32.6 us
    dot_general x4, matrix products, layer(): jnp.einsum('ekj,ekc->ejc', wig, mixed, preferred_element_type=jnp.float32)  11 us
    dot_general x2, local copies, waits for them, and re-layouts, layer(): jnp.einsum('ekj,ekc->ejc', wig, mixed, preferred_element_type=jnp.float32)  9.9 us
    dot_general x4, matrix products, layer(): jnp.dot(scatter, message.reshape(edges, coef * chan), precision=lax.Preci...  7.96 us
    another operation x2, local copies, waits for them, and re-layouts, local(): grad = jnp.stack([pack(grad_first), pack(grad_second)])  7.46 us
    reshape x2, local copies, waits for them, and re-layouts, layer(): xs = xs.astype(jnp.bfloat16).reshape(edges, coef, chan)  6.81 us
    dot_general x10, matrix products, layer(): yplus = dot(aplus, wreal) - dot(aminus, wimag)  5.89 us

commit v1 on v0

--- a/solution.py
+++ b/solution.py
@@ -304,37 +304,234 @@
     )(grad)
 
 
-def layer(x, weights, wig, rad, gather, scatter):
-    nat, coef, chan = x.shape
-    wzero, wreal, wimag = weights
-    rows = wig.shape[1]
+def mix(source, wig, outputs, inputs, coef, transposed, chan, edges, write):
+    tall = 16
+    wide = LANES if edges % LANES == 0 else edges
+    across = edges // wide
+
+    def one(number, carry):
+        t, h = number // across, lax.rem(number, across)
+        cols = pl.ds(pl.multiple_of(h * wide, wide), wide)
+        tiles = [
+            source[pl.ds(pl.multiple_of(i * chan + t * tall, tall), tall), cols]
+            for i in range(inputs)
+        ]
+        for o in range(outputs):
+            total = None
+            for i in range(inputs):
+                row = i * coef + o if transposed else o * coef + i
+                term = wig[pl.ds(row, 1), cols] * tiles[i]
+                total = term if total is None else total + term
+            write(o, pl.multiple_of(t * tall, tall), cols, total)
+        return carry
+
+    lax.fori_loop(0, (chan // tall) * across, one, 0)
+
+
+def dot(a, b, over=(1, 0)):
+    return lax.dot_general(
+        a, b, (((over[0],), (over[1],)), ((), ())), preferred_element_type=jnp.float32
+    )
+
+
+def compute_kernel(
+    shape, count_ref, x_ref, cot_ref, wig_ref, rad_ref, src_ref, dst_ref, flat_ref, grad_ref,
+    rows_f, wzero, wreal, wimag, edge_f, edge_g, rotated, small_f, outs, hidden, back, dnode, dmix,
+):
+    nat, coef, chan, rows, edges = shape
     lone = (rows + 2) // 3
-    lmore = lone - 1
-    edges = gather.shape[0]
-    kzero, kone = lone * chan, lmore * chan
-    xs = jnp.dot(gather, x.reshape(nat, coef * chan), preferred_element_type=jnp.float32)
-    xs = xs.astype(jnp.bfloat16).reshape(edges, coef, chan)
-    rot = jnp.einsum("ekj,ejc->ekc", wig, xs, preferred_element_type=jnp.float32)
-    rot = (rot * rad.astype(jnp.float32)[:, None, :]).astype(jnp.bfloat16)
-    azero = rot[:, :lone].reshape(edges, kzero)
-    aplus = rot[:, lone : lone + lmore].reshape(edges, kone)
-    aminus = rot[:, lone + lmore :].reshape(edges, kone)
-    dot = functools.partial(jnp.dot, preferred_element_type=jnp.float32)
-    yzero = dot(azero, wzero)
-    yplus = dot(aplus, wreal) - dot(aminus, wimag)
-    yminus = dot(aplus, wimag) + dot(aminus, wreal)
-    mixed = jnp.concatenate([yzero, yplus, yminus], axis=1).astype(jnp.bfloat16)
-    mixed = mixed.reshape(edges, rows, chan)
-    message = jnp.einsum("ekj,ekc->ejc", wig, mixed, preferred_element_type=jnp.float32)
-    summed = jnp.dot(scatter, message.reshape(edges, coef * chan), precision=lax.Precision.HIGH)
-    aggregated = summed.reshape(nat, coef, chan) / AVG
-    out = x.astype(jnp.float32) + aggregated
-    scalar = out[:, 0, :]
-    gated = jnp.concatenate(
-        [jax.nn.silu(scalar)[:, None, :], out[:, 1:, :] * jax.nn.sigmoid(scalar)[:, None, :]],
-        axis=1,
-    )
-    return gated.astype(jnp.bfloat16)
+    kzero, kone = lone * chan, (lone - 1) * chan
+    atoms = lax.broadcasted_iota(jnp.int32, (nat, edges), 0)
+    slots = lax.broadcasted_iota(jnp.int32, (nat, edges), 1)
+    take = (src_ref[...] == atoms).astype(jnp.float32).astype(jnp.bfloat16)
+    live = (dst_ref[...] == atoms) & (slots < count_ref[0])
+    put = live.astype(jnp.float32).astype(jnp.bfloat16)
+
+    def per_coef(body):
+        def one(j, carry):
+            body(pl.ds(pl.multiple_of(j * chan, chan), chan))
+            return carry
+
+        lax.fori_loop(0, coef, one, 0)
+
+    def blocks():
+        cut = kzero * kzero // LANES
+        step = kone * kone // LANES
+        return ((wzero, 0, kzero), (wreal, cut, kone), (wimag, cut + step, kone))
+
+    def load_weights(layer):
+        rows_f[...] = flat_ref[layer].astype(jnp.float32)
+        for ref, start, size in blocks():
+            per = size // LANES
+            for c in range(per):
+                ref[:, c * LANES : (c + 1) * LANES] = rows_f[
+                    pl.ds(start + c, size, stride=per), :
+                ].astype(jnp.bfloat16)
+
+    def store_grads(layer, grads):
+        for (_, start, size), grad in zip(blocks(), grads):
+            per = size // LANES
+            value = grad()
+            for c in range(per):
+                rows_f[pl.ds(start + c, size, stride=per), :] = value[
+                    :, c * LANES : (c + 1) * LANES
+                ]
+        grad_ref[layer] = rows_f[...].astype(jnp.bfloat16)
+
+    def forward(layer, node, last):
+        def pick(at):
+            edge_f[at, :] = dot(node[at, :], take)
+
+        per_coef(pick)
+
+        def write(o, t, cols, total):
+            scaled = total * rad_ref[layer, pl.ds(t, 16), cols].astype(jnp.float32)
+            rotated[layer, pl.ds(o * chan + t, 16), cols] = scaled.astype(jnp.bfloat16)
+
+        mix(edge_f, wig_ref, rows, coef, coef, False, chan, edges, write)
+        azero = rotated[layer, :kzero]
+        aplus = rotated[layer, kzero : kzero + kone]
+        aminus = rotated[layer, kzero + kone :]
+
+        def rounded(value):
+            return value.astype(jnp.bfloat16).astype(jnp.float32)
+
+        small_f[:kzero] = rounded(dot(wzero[...], azero, (0, 0)))
+        small_f[kzero : kzero + kone] = rounded(
+            dot(wreal[...], aplus, (0, 0)) - dot(wimag[...], aminus, (0, 0))
+        )
+        small_f[kzero + kone :] = rounded(
+            dot(wimag[...], aplus, (0, 0)) + dot(wreal[...], aminus, (0, 0))
+        )
+
+        def message(o, t, cols, total):
+            edge_g[pl.ds(o * chan + t, 16), cols] = total
+
+        mix(small_f, wig_ref, coef, rows, coef, True, chan, edges, message)
+
+        def gathered(at):
+            value = edge_g[at, :]
+            high = value.astype(jnp.bfloat16)
+            low = (value - high.astype(jnp.float32)).astype(jnp.bfloat16)
+            total = dot(high, put, (1, 1)) + dot(low, put, (1, 1))
+            outs[layer, at, :] = node[at, :].astype(jnp.float32) + total / AVG
+
+        per_coef(gathered)
+        if last:
+            return
+        gate = jax.nn.sigmoid(outs[layer, :chan, :])
+
+        def activate(at):
+            hidden[at, :] = (outs[layer, at, :] * gate).astype(jnp.bfloat16)
+
+        per_coef(activate)
+
+    def backward(layer, cot, last):
+        scalar = outs[layer, :chan, :]
+        gate = jax.nn.sigmoid(scalar)
+        slope = gate * (1.0 - gate)
+
+        def one(j, total):
+            at = pl.ds(pl.multiple_of(j * chan, chan), chan)
+            value = cot[at, :].astype(jnp.float32)
+            dnode[at, :] = value * gate
+            return total + value * outs[layer, at, :]
+
+        total = lax.fori_loop(1, coef, one, jnp.zeros((chan, nat), jnp.float32))
+        lead = cot[:chan, :].astype(jnp.float32)
+        dnode[:chan, :] = lead * (gate + scalar * slope) + total * slope
+
+        def spread(at):
+            value = dnode[at, :] / AVG
+            high = value.astype(jnp.bfloat16)
+            low = (value - high.astype(jnp.float32)).astype(jnp.bfloat16)
+            edge_f[at, :] = dot(high, put) + dot(low, put)
+
+        per_coef(spread)
+
+        def write(o, t, cols, total):
+            dmix[pl.ds(o * chan + t, 16), cols] = total.astype(jnp.bfloat16)
+
+        mix(edge_f, wig_ref, rows, coef, coef, False, chan, edges, write)
+        dzero = dmix[:kzero]
+        dplus = dmix[kzero : kzero + kone]
+        dminus = dmix[kzero + kone :]
+        azero = rotated[layer, :kzero]
+        aplus = rotated[layer, kzero : kzero + kone]
+        aminus = rotated[layer, kzero + kone :]
+        store_grads(
+            layer,
+            (
+                lambda: dot(azero, dzero, (1, 1)),
+                lambda: dot(aplus, dplus, (1, 1)) + dot(aminus, dminus, (1, 1)),
+                lambda: dot(aplus, dminus, (1, 1)) - dot(aminus, dplus, (1, 1)),
+            ),
+        )
+        if last:
+            return
+
+        def scaled(value):
+            value = value.astype(jnp.bfloat16).astype(jnp.float32)
+            scale = rad_ref[layer].astype(jnp.float32)
+            parts = value.shape[0] // chan
+            return jnp.concatenate(
+                [value[k * chan : (k + 1) * chan] * scale for k in range(parts)], axis=0
+            )
+
+        small_f[:kzero] = scaled(dot(wzero[...], dzero))
+        small_f[kzero : kzero + kone] = scaled(
+            dot(wreal[...], dplus) + dot(wimag[...], dminus)
+        )
+        small_f[kzero + kone :] = scaled(dot(wreal[...], dminus) - dot(wimag[...], dplus))
+
+        def spill(o, t, cols, total):
+            edge_g[pl.ds(o * chan + t, 16), cols] = total
+
+        mix(small_f, wig_ref, coef, rows, coef, True, chan, edges, spill)
+
+        def collect(at):
+            value = edge_g[at, :].astype(jnp.bfloat16)
+            back[at, :] = (dnode[at, :] + dot(value, take, (1, 1))).astype(jnp.bfloat16)
+
+        per_coef(collect)
+
+    load_weights(0)
+    forward(0, x_ref, False)
+    load_weights(1)
+    forward(1, hidden, True)
+    backward(1, cot_ref, False)
+    backward(0, back, True)
+
+
+def device_grads(count, feats, cot, wig, rad, src, dst, flat, shape):
+    nat, coef, chan, rows, edges = shape
+    lone = (rows + 2) // 3
+    kzero, kone = lone * chan, (lone - 1) * chan
+    wide = coef * chan
+    vmem = pl.BlockSpec(memory_space=pltpu.VMEM)
+    return pl.pallas_call(
+        functools.partial(compute_kernel, shape),
+        out_shape=jax.ShapeDtypeStruct(flat.shape, jnp.bfloat16),
+        in_specs=[pl.BlockSpec(memory_space=pltpu.SMEM)] + [vmem] * 7,
+        out_specs=vmem,
+        scratch_shapes=[
+            pltpu.VMEM(flat.shape[1:], jnp.float32),
+            pltpu.VMEM((kzero, kzero), jnp.bfloat16),
+            pltpu.VMEM((kone, kone), jnp.bfloat16),
+            pltpu.VMEM((kone, kone), jnp.bfloat16),
+            pltpu.VMEM((wide, edges), jnp.float32),
+            pltpu.VMEM((wide, edges), jnp.float32),
+            pltpu.VMEM((2, rows * chan, edges), jnp.bfloat16),
+            pltpu.VMEM((rows * chan, edges), jnp.float32),
+            pltpu.VMEM((2, wide, nat), jnp.float32),
+            pltpu.VMEM((wide, nat), jnp.bfloat16),
+            pltpu.VMEM((wide, nat), jnp.bfloat16),
+            pltpu.VMEM((wide, nat), jnp.float32),
+            pltpu.VMEM((rows * chan, edges), jnp.bfloat16),
+        ],
+        compiler_params=pltpu.CompilerParams(vmem_limit_bytes=56 << 20),
+        name="device_grads",
+    )(count, feats, cot, wig, rad, src, dst, flat)
 
 
 def local(
@@ -356,40 +553,22 @@
     else:
         full = full.reshape(layers, shards, padded)[:, :, :length]
     full = full.reshape(layers, shards * length // LANES, LANES)
-    lone = (wigner.shape[0] + 2) // 3
-    kzero, kone = lone * chan, (lone - 1) * chan
-    cut = kzero * kzero // LANES
-    step = kone * kone // LANES
-
-    def unpack(flat):
-        return (
-            flat[:cut].reshape(kzero, kzero),
-            flat[cut : cut + step].reshape(kone, kone),
-            flat[cut + step :].reshape(kone, kone),
-        )
-
-    def pack(grads):
-        return jnp.concatenate([g.reshape(-1, LANES) for g in grads], axis=0)
-
     edges = edge_src.shape[0]
-    atoms = jnp.arange(nat, dtype=jnp.int32)
-    valid = jnp.arange(edges, dtype=jnp.int32) < edge_count[0]
-    gather = (edge_src[:, None] == atoms[None, :]).astype(jnp.bfloat16)
-    scatter = jnp.where(valid[None, :], edge_dst[None, :] == atoms[:, None], False)
-    scatter = scatter.astype(jnp.float32)
-    wig = jnp.transpose(wigner, (2, 0, 1))
-
-    def first(wts):
-        return layer(node_feats, wts, wig, radial[0], gather, scatter)
-
-    def second(hidden, wts):
-        return layer(hidden, wts, wig, radial[1], gather, scatter)
-
-    hidden, pull_first = jax.vjp(first, unpack(full[0]))
-    _, pull_second = jax.vjp(second, hidden, unpack(full[1]))
-    back, grad_second = pull_second(cotangent)
-    (grad_first,) = pull_first(back)
-    grad = jnp.stack([pack(grad_first), pack(grad_second)])
+
+    def turned(nodes):
+        return jnp.transpose(nodes.reshape(nat, coef * chan))
+
+    grad = device_grads(
+        edge_count,
+        turned(node_feats),
+        turned(cotangent),
+        wigner.reshape(-1, edges).astype(jnp.float32),
+        jnp.transpose(radial, (0, 2, 1)),
+        edge_src[None, :],
+        edge_dst[None, :],
+        full,
+        (nat, coef, chan, wigner.shape[0], edges),
+    )
     if length % LANES == 0:
         grad = grad.reshape(layers, shards, length // LANES, LANES)
         grad = jnp.pad(grad, ((0, 0), (0, 0), (0, rows - length // LANES), (0, 0)))

time: 207 us -> 155 us (0.75)
  Pallas kernels: 66.5 us -> 129 us
  local copies, waits for them, and re-layouts: 78.9 us -> 21.2 us
  matrix products: 45.4 us -> 0 us
  other arithmetic: 12.3 us -> 2.63 us
    pallas_call x0 -> x1, Pallas kernels: none -> 62.6 us  [device_grads(): pl.pallas_call(functools.partial(compute_kernel, shape), out_shape=jax.Sh...]
    dot_general x39 -> x0, matrix products: 45.4 us -> none  [the longest x4 11 us: layer(): jnp.einsum('ekj,ekc->ejc', wig, mixed, preferred_element_type=jnp.float32)]
    convert_element_type x9 -> x2, local copies, waits for them, and re-layouts: 16.5 us -> 0.86 us  [local(): wigner.reshape(-1, edges).astype(jnp.float32)]
    slice x14 -> x1, local copies, waits for them, and re-layouts: 13.3 us -> 2.1 us  [local(): full = full[:, :, :length // LANES]]
    dot_general x2 -> x0, local copies, waits for them, and re-layouts: 9.9 us -> none  [layer(): jnp.einsum('ekj,ekc->ejc', wig, mixed, preferred_element_type=jnp.float32)]
    reshape x16 -> x2, local copies, waits for them, and re-layouts: 20.3 us -> 12.3 us  [the longest x1 6.21 us: local(): full = full.reshape(layers, shards * length // LANES, LANES)]
    another operation x2 -> x0, local copies, waits for them, and re-layouts: 7.46 us -> none  [local(): grad = jnp.stack([pack(grad_first), pack(grad_second)])]
    concatenate x4 -> x0, other arithmetic: 5.05 us -> none  [the longest x2 3.87 us: pack(): return jnp.concatenate([g.reshape(-1, LANES) for g in grads], axis=0)]
where the time goes in v1:
time: 155 us; the launch traced here: 154 us
  Pallas kernels  129 us (83%)
  local copies, waits for them, and re-layouts  21.2 us (14%)
  other arithmetic  2.63 us (2%)
    pallas_call x1, Pallas kernels, device_grads(): pl.pallas_call(functools.partial(compute_kernel, shape), out_shape=jax.Sh...  62.6 us
    pallas_call x1, Pallas kernels, gather_shards(): pl.pallas_call(functools.partial(gather_kernel, dims), out_shape=jax.Shap...  33.8 us
    pallas_call x1, Pallas kernels, reduce_shards(): pl.pallas_call(functools.partial(reduce_kernel, dims), out_shape=jax.Shap...  32.6 us
    reshape x1, local copies, waits for them, and re-layouts, local(): full = full.reshape(layers, shards * length // LANES, LANES)  6.21 us
    reshape x1, local copies, waits for them, and re-layouts, local(): grad = grad.reshape(layers, shards, length // LANES, LANES)  6.13 us
    unnamed x20, local copies, waits for them, and re-layouts  3.52 us

profile of v1, /device:TPU:0, one launch (start us, length us, event | category | flops | bytes accessed | tf_op | source)
XLA Modules:
  0.0 154.2 jit_solution(9111436072427769013)
XLA Ops:
  0.6 1.0 convert_element_type.14
  1.7 0.1 pad_bitcast_fusion
  1.8 33.8 %gather_shards.1 = bf16[2,4,2,2,2,240,128]{6,5,4,3,2,1,0:T(8,128)(2,1)S(1)} custom-call(bf16[2,240,128]{2,1,0:T(8,128)(2,1)S(1)} %bitcast.23), custom_call_target="tpu_custom_call" | custom-call | tf_op jit(solution)/shard_map/gather_shards/pallas_call | solution.py:128
  35.6 2.1 %slice.8 = bf16[2,32,228,128]{3,2,1,0:T(8,128)(2,1)} slice(bf16[2,32,240,128]{3,2,1,0:T(8,128)(2,1)S(1)} %bitcast.21), slice={[0:2], [0:32], [0:228], [0:128]} | slice | bytes 7471104 | tf_op jit(solution)/shard_map/slice | solution.py:552
  37.8 6.2 %reshape.37.flat_ref = bf16[2,7296,128]{2,1,0:T(8,128)(2,1)} reshape(bf16[2,32,228,128]{3,2,1,0:T(8,128)(2,1)} %slice.8) | data formatting | bytes 7471104 | tf_op jit(solution)/shard_map/reshape | solution.py:555
  44.0 0.0 copy-done.4
  44.0 1.2 copy.17
  45.2 0.0 copy-done.5
  45.2 1.2 copy.18
  46.4 0.0 copy-done.3
  46.5 0.1 copy.19
  46.5 0.8 reshape.41.wig_ref
  47.3 0.0 copy-done.6
  47.3 0.8 copy.20
  48.7 62.6 %device_grads.1 = bf16[2,7296,128]{2,1,0:T(8,128)(2,1)} custom-call(s32[1]{0:T(128)S(6)} %copy.27.count_ref, bf16[3200,24]{1,0:T(8,128)(2,1)} %bitcast.24, bf16[3200,24]{1,0:T(8,128)(2,1)} %bitcast.25, f32[325,256]{1,0:T(8,128)} %reshape.41.wig_ref, bf16[2,128,256]{2,1,0:T(8,128)(2,1)} %bitcast.27, s32[1,256]{1,0:T(1,128)} %bitcast.28, s32[1,256]{1,0:T(1,128)} %bitcast.29, ...), custom_call_target="tpu_custom_call" | custom-call | tf_op jit(solution)/shard_map/device_grads/pallas_call | solution.py:512
  111.3 6.1 %reshape.38 = bf16[2,32,228,128]{3,2,1,0:T(8,128)(2,1)} reshape(bf16[2,7296,128]{2,1,0:T(8,128)(2,1)} %device_grads.1) | data formatting | bytes 7471104 | tf_op jit(solution)/shard_map/reshape | solution.py:573
  117.4 2.3 %pad.9 = bf16[2,32,240,128]{3,2,1,0:T(8,128)(2,1)S(1)} pad(bf16[2,32,228,128]{3,2,1,0:T(8,128)(2,1)} %reshape.38, bf16[]{:T(256)} %constant.4.clone.1), padding=0_0x0_0x0_12x0_0 | pad | bytes 7667714 | tf_op jit(solution)/shard_map/jit(_pad)/pad | solution.py:574
  119.8 0.0 copy-start
  119.8 0.0 copy-start.1
  119.8 0.0 copy-start.2
  119.8 32.6 %reduce_shards.1 = f32[2,240,128]{2,1,0:T(8,128)S(1)} custom-call(bf16[2,4,2,2,2,240,128]{6,5,4,3,2,1,0:T(8,128)(2,1)S(1)} %bitcast.20), custom_call_target="tpu_custom_call" | custom-call | tf_op jit(solution)/shard_map/reduce_shards/pallas_call | solution.py:292
  152.4 0.1 copy.25
  152.6 0.0 copy-done
  152.6 1.6 %multiply_subtract_fusion = (f32[2,29184]{1,0:T(2,128)}, f32[2,29184]{1,0:T(2,128)}, f32[2,29184]{1,0:T(2,128)}) fusion(f32[2,29184]{1,0:T(2,128)S(1)} %copy-done, f32[2,30720]{1,0:T(2,128)S(1)} %bitcast.26, f32[2,29184]{1,0:T(2,128)S(1)} %copy-done.1, f32[2,29184]{1,0:T(2,128)S(1)} %copy-done.2), kind=kLoop, calls=%fused_computation.3 | loop fusion | flops 875520 | bytes 1634304 | tf_op jit(solution)/shard_map/sub | solution.py:584
  (7 shorter events, 0.0 us)
Async XLA Ops:
  37.7 6.2 %copy-start.4 = (bf16[24,25,128]{2,0,1:T(8,128)(2,1)S(1)}, bf16[24,25,128]{2,0,1:T(8,128)(2,1)}, u32[]{:S(2)}) copy-start(bf16[24,25,128]{2,0,1:T(8,128)(2,1)} %param.10) | copy-start | bytes 460804
  37.8 7.4 %copy-start.5 = (bf16[24,25,128]{2,0,1:T(8,128)(2,1)S(1)}, bf16[24,25,128]{2,0,1:T(8,128)(2,1)}, u32[]{:S(2)}) copy-start(bf16[24,25,128]{2,0,1:T(8,128)(2,1)} %param.11) | copy-start | bytes 460804
  37.8 8.7 %copy-start.3 = (bf16[13,25,256]{2,0,1:T(8,128)(2,1)S(1)}, bf16[13,25,256]{2,0,1:T(8,128)(2,1)}, u32[]{:S(2)}) copy-start(bf16[13,25,256]{2,0,1:T(8,128)(2,1)} %param.12) | copy-start | bytes 499204
  37.8 9.6 %copy-start.6 = (bf16[2,256,128]{2,1,0:T(8,128)(2,1)S(1)}, bf16[2,256,128]{2,1,0:T(8,128)(2,1)}, u32[]{:S(2)}) copy-start(bf16[2,256,128]{2,1,0:T(8,128)(2,1)} %param.13) | copy-start | bytes 393220
  119.8 32.8 %copy-start = (f32[2,29184]{1,0:T(2,128)S(1)}, f32[2,29184]{1,0:T(2,128)}, u32[]{:S(2)}) copy-start(f32[2,29184]{1,0:T(2,128)} %param.17) | copy-start | bytes 700420
  119.8 32.8 %copy-start.1 = (f32[2,29184]{1,0:T(2,128)S(1)}, f32[2,29184]{1,0:T(2,128)}, u32[]{:S(2)}) copy-start(f32[2,29184]{1,0:T(2,128)} %param.18) | copy-start | bytes 700420
  119.8 32.8 %copy-start.2 = (f32[2,29184]{1,0:T(2,128)S(1)}, f32[2,29184]{1,0:T(2,128)}, u32[]{:S(2)}) copy-start(f32[2,29184]{1,0:T(2,128)} %param.19) | copy-start | bytes 700420

commit v2 on v1

--- a/solution.py
+++ b/solution.py
@@ -61,15 +61,16 @@
     pl.semaphore_wait(barrier, count)
 
 
-def gather_kernel(dims, own_ref, out_ref, local_sem, send_sem, recv_sem):
-    me = place(dims)
+def gather_steps(dims, me, own_ref, out_ref, local_sem, send_sem, recv_sem):
     layers, rows = own_ref.shape[0], own_ref.shape[1]
     part = rows // PIECES
-    greet(dims, me)
     mine = pltpu.make_async_copy(
         own_ref, out_ref.at[:, me["z"], me["y"], me["c"], me["x"]], local_sem
     )
     mine.start()
+    most = max(size_of(dims, a) for a in "zyxc") - 1
+    started = {}
+    state = {"mine": True}
 
     def view(ref, layer, piece, spans, at):
         index = [layer]
@@ -78,20 +79,19 @@
         index.append(pl.ds(piece * part, part))
         return ref.at[tuple(index)]
 
-    items = []
-    for layer in range(layers):
+    def advance(layer, phase):
         for piece in range(PIECES):
-            order = "zyxc" if (layer * PIECES + piece) % 2 == 0 else "zxyc"
-            items.append((layer, piece, order))
-    most = max(size_of(dims, a) for a in "zyxc") - 1
-    started = []
-    for phase in range(4):
-        for number, (layer, piece, order) in enumerate(items):
-            spans = order[:phase]
+            number = layer * PIECES + piece
+            order = "zyxc" if number % 2 == 0 else "zxyc"
             if phase:
-                for copy in started[(phase - 1) * len(items) + number]:
+                for copy in started[number, phase - 1]:
                     copy.wait_recv()
-            axis = order[phase]
+                if state["mine"]:
+                    mine.wait()
+                    state["mine"] = False
+            if phase == 4:
+                continue
+            axis, spans = order[phase], order[:phase]
             copies = []
             for step in range(1, size_of(dims, axis)):
                 if phase == 0:
@@ -109,15 +109,24 @@
                 )
                 copy.start()
                 copies.append(copy)
-            started.append(copies)
-        if phase == 0:
-            mine.wait()
-    for copies in started[3 * len(items) :]:
-        for copy in copies:
-            copy.wait_recv()
-    for copies in started:
-        for copy in copies:
-            copy.wait_send()
+            started[number, phase] = copies
+
+    def finish():
+        for copies in started.values():
+            for copy in copies:
+                copy.wait_send()
+
+    return advance, finish
+
+
+def gather_kernel(dims, own_ref, out_ref, local_sem, send_sem, recv_sem):
+    me = place(dims)
+    greet(dims, me)
+    advance, finish = gather_steps(dims, me, own_ref, out_ref, local_sem, send_sem, recv_sem)
+    for phase in range(5):
+        for layer in range(own_ref.shape[0]):
+            advance(layer, phase)
+    finish()
 
 
 def gather_shards(dims, own, collective_id):
@@ -170,14 +179,12 @@
     return items
 
 
-def reduce_kernel(dims, grad_ref, out_ref, pair_buf, *scratch):
+def reduce_steps(dims, me, grad_ref, out_ref, pair_buf, scratch):
     zs = dims[0]
     buffers = (scratch[:9], scratch[9:18])
-    send_sem, recv_sem = scratch[18:]
-    me = place(dims)
+    send_sem, recv_sem = scratch[18:20]
     layers, rows = out_ref.shape[0], out_ref.shape[1]
     part = rows // PIECES
-    greet(dims, me)
     items = reduce_items(layers)
     most = max(size_of(dims, a) for a in "zyxc") - 1
     pending = []
@@ -200,16 +207,21 @@
         return value.astype(jnp.float32)
 
     waits = {}
-    for number, (layer, piece, kind, place_in) in enumerate(items):
-        span = pl.ds(piece * part, part)
-        waits[number] = [
-            send(
-                number, 0, 1, "c",
-                grad_ref.at[layer, :, :, 1 - me["c"], :, span], pair_buf.at[number],
-            )
-        ]
-    for phase in range(4):
+
+    def advance(wanted, now):
+        phase = now - 1
         for number, (layer, piece, kind, place_in) in enumerate(items):
+            if layer != wanted:
+                continue
+            if now == 0:
+                waits[number] = [
+                    send(
+                        number, 0, 1, "c",
+                        grad_ref.at[layer, :, :, 1 - me["c"], :, pl.ds(piece * part, part)],
+                        pair_buf.at[number],
+                    )
+                ]
+                continue
             span = pl.ds(piece * part, part)
             acc1, send1, recv1, acc2, send2, recv2, acc3, send3, recv3 = (
                 buf.at[place_in] for buf in buffers[kind]
@@ -278,25 +290,32 @@
                     total = total + f32(recv3[e])
                 out_ref[layer, span] = total
             waits[number] = copies
-    for copy in pending:
-        copy.wait_send()
+
+    def finish():
+        for copy in pending:
+            copy.wait_send()
+
+    return advance, finish
+
+
+def reduce_kernel(dims, grad_ref, out_ref, pair_buf, *scratch):
+    me = place(dims)
+    greet(dims, me)
+    advance, finish = reduce_steps(dims, me, grad_ref, out_ref, pair_buf, scratch)
+    for phase in range(5):
+        for layer in reversed(range(out_ref.shape[0])):
+            advance(layer, phase)
+    finish()
 
 
 def reduce_shards(dims, grad, collective_id):
-    layers, zs, ys, _, xs, rows, lanes = grad.shape
-    part = rows // PIECES
-    most = max(zs, ys, xs, 2) - 1
-    count = layers * PIECES
-    slots = count * 4 * most
-    even, odd = (count + 1) // 2, count // 2
+    layers, _, _, _, _, rows, lanes = grad.shape
     return pl.pallas_call(
         functools.partial(reduce_kernel, dims),
         out_shape=jax.ShapeDtypeStruct((layers, rows, lanes), jnp.float32),
         in_specs=[pl.BlockSpec(memory_space=pltpu.VMEM)],
         out_specs=pl.BlockSpec(memory_space=pltpu.VMEM),
-        scratch_shapes=[pltpu.VMEM((count, zs, ys, xs, part, lanes), grad.dtype)]
-        + reduce_buffers(dims, (("x", "y", even), ("y", "x", odd)), part)
-        + [pltpu.SemaphoreType.DMA((slots,)), pltpu.SemaphoreType.DMA((slots,))],
+        scratch_shapes=reduce_scratch(dims, layers, rows),
         compiler_params=pltpu.CompilerParams(
             collective_id=collective_id, has_side_effects=True, vmem_limit_bytes=48 << 20
         ),
@@ -304,7 +323,7 @@
     )(grad)
 
 
-def mix(source, wig, outputs, inputs, coef, transposed, chan, edges, write):
+def mix(source, wig, outputs, inputs, coef, transposed, chan, edges, write, hooks=()):
     tall = 16
     wide = LANES if edges % LANES == 0 else edges
     across = edges // wide
@@ -325,7 +344,12 @@
             write(o, pl.multiple_of(t * tall, tall), cols, total)
         return carry
 
-    lax.fori_loop(0, (chan // tall) * across, one, 0)
+    total = (chan // tall) * across
+    spans = len(hooks) + 1
+    for n in range(spans):
+        lax.fori_loop(n * total // spans, (n + 1) * total // spans, one, 0)
+        if n < len(hooks):
+            hooks[n]()
 
 
 def dot(a, b, over=(1, 0)):
@@ -336,8 +360,23 @@
 
 def compute_kernel(
     shape, count_ref, x_ref, cot_ref, wig_ref, rad_ref, src_ref, dst_ref, flat_ref, grad_ref,
-    rows_f, wzero, wreal, wimag, edge_f, edge_g, rotated, small_f, outs, hidden, back, dnode, dmix,
+    *scratch,
 ):
+    rows_f = scratch[0]
+
+    def unpack(layer):
+        rows_f[...] = flat_ref[layer].astype(jnp.float32)
+
+    def pack(layer):
+        grad_ref[layer] = rows_f[...].astype(jnp.bfloat16)
+
+    refs = (count_ref, x_ref, cot_ref, wig_ref, rad_ref, src_ref, dst_ref)
+    compute(shape, refs, scratch, unpack, pack, lambda *step: None, lambda *step: None)
+
+
+def compute(shape, refs, scratch, unpack, pack, gather, reduce):
+    count_ref, x_ref, cot_ref, wig_ref, rad_ref, src_ref, dst_ref = refs
+    (rows_f, wzero, wreal, wimag, edge_f, edge_g, rotated, small_f, outs, hidden, back, dnode, dmix) = scratch
     nat, coef, chan, rows, edges = shape
     lone = (rows + 2) // 3
     kzero, kone = lone * chan, (lone - 1) * chan
@@ -360,7 +399,7 @@
         return ((wzero, 0, kzero), (wreal, cut, kone), (wimag, cut + step, kone))
 
     def load_weights(layer):
-        rows_f[...] = flat_ref[layer].astype(jnp.float32)
+        unpack(layer)
         for ref, start, size in blocks():
             per = size // LANES
             for c in range(per):
@@ -376,9 +415,9 @@
                 rows_f[pl.ds(start + c, size, stride=per), :] = value[
                     :, c * LANES : (c + 1) * LANES
                 ]
-        grad_ref[layer] = rows_f[...].astype(jnp.bfloat16)
-
-    def forward(layer, node, last):
+        pack(layer)
+
+    def forward(layer, node, last, early, late):
         def pick(at):
             edge_f[at, :] = dot(node[at, :], take)
 
@@ -388,7 +427,9 @@
             scaled = total * rad_ref[layer, pl.ds(t, 16), cols].astype(jnp.float32)
             rotated[layer, pl.ds(o * chan + t, 16), cols] = scaled.astype(jnp.bfloat16)
 
-        mix(edge_f, wig_ref, rows, coef, coef, False, chan, edges, write)
+        mix(edge_f, wig_ref, rows, coef, coef, False, chan, edges, write, early)
+        gather(layer, 4)
+        load_weights(layer)
         azero = rotated[layer, :kzero]
         aplus = rotated[layer, kzero : kzero + kone]
         aminus = rotated[layer, kzero + kone :]
@@ -407,7 +448,7 @@
         def message(o, t, cols, total):
             edge_g[pl.ds(o * chan + t, 16), cols] = total
 
-        mix(small_f, wig_ref, coef, rows, coef, True, chan, edges, message)
+        mix(small_f, wig_ref, coef, rows, coef, True, chan, edges, message, late)
 
         def gathered(at):
             value = edge_g[at, :]
@@ -426,7 +467,7 @@
 
         per_coef(activate)
 
-    def backward(layer, cot, last):
+    def backward(layer, cot, last, early, late):
         scalar = outs[layer, :chan, :]
         gate = jax.nn.sigmoid(scalar)
         slope = gate * (1.0 - gate)
@@ -452,7 +493,7 @@
         def write(o, t, cols, total):
             dmix[pl.ds(o * chan + t, 16), cols] = total.astype(jnp.bfloat16)
 
-        mix(edge_f, wig_ref, rows, coef, coef, False, chan, edges, write)
+        mix(edge_f, wig_ref, rows, coef, coef, False, chan, edges, write, early)
         dzero = dmix[:kzero]
         dplus = dmix[kzero : kzero + kone]
         dminus = dmix[kzero + kone :]
@@ -467,6 +508,7 @@
                 lambda: dot(aplus, dminus, (1, 1)) - dot(aminus, dplus, (1, 1)),
             ),
         )
+        reduce(layer, 0)
         if last:
             return
 
@@ -487,7 +529,7 @@
         def spill(o, t, cols, total):
             edge_g[pl.ds(o * chan + t, 16), cols] = total
 
-        mix(small_f, wig_ref, coef, rows, coef, True, chan, edges, spill)
+        mix(small_f, wig_ref, coef, rows, coef, True, chan, edges, spill, late)
 
         def collect(at):
             value = edge_g[at, :].astype(jnp.bfloat16)
@@ -495,43 +537,148 @@
 
         per_coef(collect)
 
-    load_weights(0)
-    forward(0, x_ref, False)
-    load_weights(1)
-    forward(1, hidden, True)
-    backward(1, cot_ref, False)
-    backward(0, back, True)
-
-
-def device_grads(count, feats, cot, wig, rad, src, dst, flat, shape):
+    def step(move, layer, phase):
+        return lambda: move(layer, phase)
+
+    forward(
+        0, x_ref, False,
+        (step(gather, 0, 1), step(gather, 0, 2), step(gather, 0, 3)),
+        (step(gather, 1, 1), step(gather, 1, 2)),
+    )
+    gather(1, 3)
+    forward(1, hidden, True, (), ())
+    backward(1, cot_ref, False, (), (step(reduce, 1, 1), step(reduce, 1, 2)))
+    reduce(1, 3)
+    backward(0, back, True, (step(reduce, 1, 4),), ())
+
+
+def fused_kernel(
+    dims, shape, length, own_ref, count_ref, x_ref, cot_ref, wig_ref, rad_ref, src_ref, dst_ref,
+    out_ref, full_ref, grad_ref, local_sem, gather_send, gather_recv, *scratch,
+):
+    zs, ys, xs = dims
+    me = place(dims)
+    greet(dims, me)
+    work, rest = scratch[:13], scratch[13:]
+    rows_f = work[0]
+    used, rows = length // LANES, own_ref.shape[1]
+    gather, gathered = gather_steps(
+        dims, me, own_ref, full_ref, local_sem, gather_send, gather_recv
+    )
+    reduce, reduced = reduce_steps(dims, me, grad_ref, out_ref, rest[0], rest[1:])
+
+    def shards():
+        number = 0
+        for z in range(zs):
+            for y in range(ys):
+                for c in range(2):
+                    for x in range(xs):
+                        yield number, (z, y, c, x)
+                        number += 1
+
+    def unpack(layer):
+        for number, at in shards():
+            rows_f[number * used : number * used + rows, :] = full_ref[(layer,) + at].astype(
+                jnp.float32
+            )
+
+    def pack(layer):
+        for number, at in shards():
+            grad_ref[(layer,) + at] = rows_f[number * used : number * used + rows, :].astype(
+                jnp.bfloat16
+            )
+
+    def moved(layer, phase):
+        gather(layer, phase)
+        if (layer, phase) == (0, 2):
+            gather(1, 0)
+
+    gather(0, 0)
+    refs = (count_ref, x_ref, cot_ref, wig_ref, rad_ref, src_ref, dst_ref)
+    compute(shape, refs, work, unpack, pack, moved, reduce)
+    for phase in range(1, 5):
+        reduce(0, phase)
+    gathered()
+    reduced()
+
+
+def work_buffers(shape, flat_rows):
     nat, coef, chan, rows, edges = shape
     lone = (rows + 2) // 3
     kzero, kone = lone * chan, (lone - 1) * chan
     wide = coef * chan
+    return [
+        pltpu.VMEM((flat_rows, LANES), jnp.float32),
+        pltpu.VMEM((kzero, kzero), jnp.bfloat16),
+        pltpu.VMEM((kone, kone), jnp.bfloat16),
+        pltpu.VMEM((kone, kone), jnp.bfloat16),
+        pltpu.VMEM((wide, edges), jnp.float32),
+        pltpu.VMEM((wide, edges), jnp.float32),
+        pltpu.VMEM((2, rows * chan, edges), jnp.bfloat16),
+        pltpu.VMEM((rows * chan, edges), jnp.float32),
+        pltpu.VMEM((2, wide, nat), jnp.float32),
+        pltpu.VMEM((wide, nat), jnp.bfloat16),
+        pltpu.VMEM((wide, nat), jnp.bfloat16),
+        pltpu.VMEM((wide, nat), jnp.float32),
+        pltpu.VMEM((rows * chan, edges), jnp.bfloat16),
+    ]
+
+
+def reduce_scratch(dims, layers, rows):
+    zs, ys, xs = dims
+    part = rows // PIECES
+    most = max(zs, ys, xs, 2) - 1
+    count = layers * PIECES
+    slots = count * 4 * most
+    even, odd = (count + 1) // 2, count // 2
+    return (
+        [pltpu.VMEM((count, zs, ys, xs, part, LANES), jnp.bfloat16)]
+        + reduce_buffers(dims, (("x", "y", even), ("y", "x", odd)), part)
+        + [pltpu.SemaphoreType.DMA((slots,)), pltpu.SemaphoreType.DMA((slots,))]
+    )
+
+
+def owned_grads(dims, own, length, inputs, shape, collective_id):
+    zs, ys, xs = dims
+    layers, rows, _ = own.shape
+    most = max(zs, ys, xs, 2) - 1
+    slots = layers * PIECES * 4 * most
+    spread = (layers, zs, ys, 2, xs, rows, LANES)
+    flat_rows = zs * ys * 2 * xs * (length // LANES)
+    flat_rows = -(-(flat_rows + rows) // 8) * 8
+    vmem = pl.BlockSpec(memory_space=pltpu.VMEM)
+    return pl.pallas_call(
+        functools.partial(fused_kernel, dims, shape, length),
+        out_shape=jax.ShapeDtypeStruct(own.shape, jnp.float32),
+        in_specs=[vmem, pl.BlockSpec(memory_space=pltpu.SMEM)] + [vmem] * 6,
+        out_specs=vmem,
+        scratch_shapes=[
+            pltpu.VMEM(spread, jnp.bfloat16),
+            pltpu.VMEM(spread, jnp.bfloat16),
+            pltpu.SemaphoreType.DMA,
+            pltpu.SemaphoreType.DMA((slots,)),
+            pltpu.SemaphoreType.DMA((slots,)),
+        ]
+        + work_buffers(shape, flat_rows)
+        + reduce_scratch(dims, layers, rows),
+        compiler_params=pltpu.CompilerParams(
+            collective_id=collective_id, has_side_effects=True, vmem_limit_bytes=60 << 20
+        ),
+        name="owned_grads",
+    )(own, *inputs)
+
+
+def device_grads(inputs, flat, shape):
     vmem = pl.BlockSpec(memory_space=pltpu.VMEM)
     return pl.pallas_call(
         functools.partial(compute_kernel, shape),
         out_shape=jax.ShapeDtypeStruct(flat.shape, jnp.bfloat16),
         in_specs=[pl.BlockSpec(memory_space=pltpu.SMEM)] + [vmem] * 7,
         out_specs=vmem,
-        scratch_shapes=[
-            pltpu.VMEM(flat.shape[1:], jnp.float32),
-            pltpu.VMEM((kzero, kzero), jnp.bfloat16),
-            pltpu.VMEM((kone, kone), jnp.bfloat16),
-            pltpu.VMEM((kone, kone), jnp.bfloat16),
-            pltpu.VMEM((wide, edges), jnp.float32),
-            pltpu.VMEM((wide, edges), jnp.float32),
-            pltpu.VMEM((2, rows * chan, edges), jnp.bfloat16),
-            pltpu.VMEM((rows * chan, edges), jnp.float32),
-            pltpu.VMEM((2, wide, nat), jnp.float32),
-            pltpu.VMEM((wide, nat), jnp.bfloat16),
-            pltpu.VMEM((wide, nat), jnp.bfloat16),
-            pltpu.VMEM((wide, nat), jnp.float32),
-            pltpu.VMEM((rows * chan, edges), jnp.bfloat16),
-        ],
+        scratch_shapes=work_buffers(shape, flat.shape[1]),
         compiler_params=pltpu.CompilerParams(vmem_limit_bytes=56 << 20),
         name="device_grads",
-    )(count, feats, cot, wig, rad, src, dst, flat)
+    )(*inputs, flat)
 
 
 def local(
@@ -546,19 +693,14 @@
     padded = -(-length // block) * block
     rows = padded // LANES
     own = jnp.pad(params.astype(jnp.bfloat16), ((0, 0), (0, padded - length)))
-    full = gather_shards(dims, own.reshape(layers, rows, LANES), 0)
-    full = full.reshape(layers, shards, rows, LANES)
-    if length % LANES == 0:
-        full = full[:, :, : length // LANES]
-    else:
-        full = full.reshape(layers, shards, padded)[:, :, :length]
-    full = full.reshape(layers, shards * length // LANES, LANES)
+    own = own.reshape(layers, rows, LANES)
     edges = edge_src.shape[0]
+    shape = (nat, coef, chan, wigner.shape[0], edges)
 
     def turned(nodes):
         return jnp.transpose(nodes.reshape(nat, coef * chan))
 
-    grad = device_grads(
+    inputs = (
         edge_count,
         turned(node_feats),
         turned(cotangent),
@@ -566,16 +708,15 @@
         jnp.transpose(radial, (0, 2, 1)),
         edge_src[None, :],
         edge_dst[None, :],
-        full,
-        (nat, coef, chan, wigner.shape[0], edges),
     )
     if length % LANES == 0:
-        grad = grad.reshape(layers, shards, length // LANES, LANES)
-        grad = jnp.pad(grad, ((0, 0), (0, 0), (0, rows - length // LANES), (0, 0)))
+        owned = owned_grads(dims, own, length, inputs, shape, 0)
     else:
-        grad = grad.reshape(layers, shards, length)
+        full = gather_shards(dims, own, 0).reshape(layers, shards, padded)[:, :, :length]
+        full = full.reshape(layers, shards * length // LANES, LANES)
+        grad = device_grads(inputs, full, shape).reshape(layers, shards, length)
         grad = jnp.pad(grad, ((0, 0), (0, 0), (0, padded - length)))
-    owned = reduce_shards(dims, grad.reshape(layers, zs, ys, 2, xs, rows, LANES), 1)
+        owned = reduce_shards(dims, grad.reshape(layers, zs, ys, 2, xs, rows, LANES), 1)
     grad = owned.reshape(layers, padded)[:, :length]
     new_moment1 = 0.9 * moment1 + 0.1 * grad
     new_moment2 = 0.95 * moment2 + 0.05 * grad * grad

time: 155 us -> 123 us (0.79)
  Pallas kernels: 129 us -> 112 us
  local copies, waits for them, and re-layouts: 21.2 us -> 6.24 us
    pallas_call x3 -> x1, Pallas kernels: 129 us -> 112 us  [owned_grads(): pl.pallas_call(functools.partial(fused_kernel, dims, shape, length), out_...]
    reshape x2 -> x0, local copies, waits for them, and re-layouts: 12.3 us -> none  [the longest x1 6.21 us: local(): full = full.reshape(layers, shards * length // LANES, LANES)]
    pad x1 -> x0, local copies, waits for them, and re-layouts: 2.35 us -> none  [local(): grad = jnp.pad(grad, ((0, 0), (0, 0), (0, rows - length // LANES), (0, 0)))]
    slice x1 -> x0, local copies, waits for them, and re-layouts: 2.1 us -> none  [local(): full = full[:, :, :length // LANES]]
    unnamed x20, local copies, waits for them, and re-layouts: 3.52 us -> 5.37 us
where the time goes in v2:
time: 123 us; the launch traced here: 122 us
  Pallas kernels  112 us (91%)
  local copies, waits for them, and re-layouts  6.24 us (5%)
  other arithmetic  2.63 us (2%)
  between operations  1.37 us (1%)
    pallas_call x1, Pallas kernels, owned_grads(): pl.pallas_call(functools.partial(fused_kernel, dims, shape, length), out_...  112 us
    unnamed x20, local copies, waits for them, and re-layouts  5.37 us

profile of v2, /device:TPU:0, one launch (start us, length us, event | category | flops | bytes accessed | tf_op | source)
XLA Modules:
  0.0 122.3 jit_solution(1582503703923105189)
XLA Ops:
  1.3 1.0 convert_element_type.10
  2.3 0.0 copy-start.6
  2.3 0.1 pad_bitcast_fusion
  2.4 0.0 copy-start.3
  2.4 0.7 copy.26
  3.1 0.1 copy-done.6
  3.2 0.8 copy.20
  4.0 0.0 copy-done.3
  4.0 0.1 copy.19
  4.1 0.0 copy-start.4
  4.1 0.8 reshape.25.wig_ref
  4.9 0.1 copy-done.4
  5.0 0.0 copy-start.5
  5.0 1.2 copy.17
  6.2 0.0 copy-done.5
  6.2 1.2 %copy.18 = bf16[24,25,128]{0,2,1:T(8,128)(2,1)} copy(bf16[24,25,128]{2,0,1:T(8,128)(2,1)S(1)} %copy-done.5) | data formatting | bytes 307200 | tf_op args[1]
  7.4 112.1 %owned_grads.1 = f32[2,240,128]{2,1,0:T(8,128)} custom-call(bf16[2,240,128]{2,1,0:T(8,128)(2,1)} %bitcast.23, s32[1]{0:T(128)S(6)} %copy.27.count_ref, bf16[3200,24]{1,0:T(8,128)(2,1)} %bitcast.18, bf16[3200,24]{1,0:T(8,128)(2,1)} %bitcast.19, f32[325,256]{1,0:T(8,128)} %reshape.25.wig_ref, bf16[2,128,256]{2,1,0:T(8,128)(2,1)} %bitcast.22, ...), custom_call_target="tpu_custom_call" | custom-call | tf_op jit(solution)/shard_map/owned_grads/pallas_call | solution.py:650
  119.5 0.0 copy-start
  119.5 0.0 copy-start.1
  119.6 1.1 copy.25
  120.7 0.0 copy-done.2
  120.7 0.0 copy-done
  120.7 0.0 copy-done.1
  120.7 1.6 %multiply_subtract_fusion = (f32[2,29184]{1,0:T(2,128)}, f32[2,29184]{1,0:T(2,128)}, f32[2,29184]{1,0:T(2,128)}) fusion(f32[2,29184]{1,0:T(2,128)S(1)} %copy-done, f32[2,30720]{1,0:T(2,128)S(1)} %bitcast.21, f32[2,29184]{1,0:T(2,128)S(1)} %copy-done.1, f32[2,29184]{1,0:T(2,128)S(1)} %copy-done.2), kind=kLoop, calls=%fused_computation.3 | loop fusion | flops 875520 | bytes 1634304 | tf_op jit(solution)/shard_map/sub | solution.py:725
  (1 shorter events, 0.0 us)
Async XLA Ops:
  2.3 0.9 copy-start.6
  2.4 1.6 %copy-start.3 = (bf16[13,25,256]{2,0,1:T(8,128)(2,1)S(1)}, bf16[13,25,256]{2,0,1:T(8,128)(2,1)}, u32[]{:S(2)}) copy-start(bf16[13,25,256]{2,0,1:T(8,128)(2,1)} %param.12) | copy-start | bytes 499204
  4.1 0.9 copy-start.4
  5.0 1.2 copy-start.5
  7.4 113.3 %copy-start.2 = (f32[2,29184]{1,0:T(2,128)S(1)}, f32[2,29184]{1,0:T(2,128)}, u32[]{:S(2)}) copy-start(f32[2,29184]{1,0:T(2,128)} %param.19) | copy-start | bytes 700420
  119.5 1.2 copy-start
  119.5 1.2 copy-start.1

commit v3 on v2

--- a/solution.py
+++ b/solution.py
@@ -82,7 +82,7 @@
     def advance(layer, phase):
         for piece in range(PIECES):
             number = layer * PIECES + piece
-            order = "zyxc" if number % 2 == 0 else "zxyc"
+            order = ("yxzc", "zyxc", "zxyc")[piece % 3]
             if phase:
                 for copy in started[number, phase - 1]:
                     copy.wait_recv()

time: 123 us -> 125 us (1.016)
  Pallas kernels: 112 us -> 114 us
    pallas_call x1, Pallas kernels: 112 us -> 114 us  [owned_grads(): pl.pallas_call(functools.partial(fused_kernel, dims, shape, length), out_...]
where the time goes in v3:
time: 125 us; the launch traced here: 124 us
  Pallas kernels  114 us (91%)
  local copies, waits for them, and re-layouts  6.24 us (5%)
  other arithmetic  2.63 us (2%)
  between operations  1.37 us (1%)
    pallas_call x1, Pallas kernels, owned_grads(): pl.pallas_call(functools.partial(fused_kernel, dims, shape, length), out_...  114 us
    unnamed x20, local copies, waits for them, and re-layouts  5.37 us

profile of v3, /device:TPU:0, one launch (start us, length us, event | category | flops | bytes accessed | tf_op | source)
XLA Modules:
  0.0 124.5 jit_solution(15354884183966608624)
XLA Ops:
  1.3 1.0 convert_element_type.10
  2.3 0.0 copy-start.6
  2.3 0.1 pad_bitcast_fusion
  2.4 0.0 copy-start.3
  2.4 0.7 copy.26
  3.1 0.1 copy-done.6
  3.2 0.8 copy.20
  4.0 0.0 copy-done.3
  4.0 0.1 copy.19
  4.1 0.0 copy-start.4
  4.1 0.8 reshape.25.wig_ref
  4.9 0.1 copy-done.4
  5.0 0.0 copy-start.5
  5.0 1.2 copy.17
  6.2 0.0 copy-done.5
  6.2 1.2 %copy.18 = bf16[24,25,128]{0,2,1:T(8,128)(2,1)} copy(bf16[24,25,128]{2,0,1:T(8,128)(2,1)S(1)} %copy-done.5) | data formatting | bytes 307200 | tf_op args[1]
  7.4 114.2 %owned_grads.1 = f32[2,240,128]{2,1,0:T(8,128)} custom-call(bf16[2,240,128]{2,1,0:T(8,128)(2,1)} %bitcast.23, s32[1]{0:T(128)S(6)} %copy.27.count_ref, bf16[3200,24]{1,0:T(8,128)(2,1)} %bitcast.18, bf16[3200,24]{1,0:T(8,128)(2,1)} %bitcast.19, f32[325,256]{1,0:T(8,128)} %reshape.25.wig_ref, bf16[2,128,256]{2,1,0:T(8,128)(2,1)} %bitcast.22, ...), custom_call_target="tpu_custom_call" | custom-call | tf_op jit(solution)/shard_map/owned_grads/pallas_call | solution.py:650
  121.7 0.0 copy-start
  121.7 0.0 copy-start.1
  121.7 1.1 copy.25
  122.8 0.0 copy-done.2
  122.8 0.0 copy-done
  122.9 0.0 copy-done.1
  122.9 1.6 %multiply_subtract_fusion = (f32[2,29184]{1,0:T(2,128)}, f32[2,29184]{1,0:T(2,128)}, f32[2,29184]{1,0:T(2,128)}) fusion(f32[2,29184]{1,0:T(2,128)S(1)} %copy-done, f32[2,30720]{1,0:T(2,128)S(1)} %bitcast.21, f32[2,29184]{1,0:T(2,128)S(1)} %copy-done.1, f32[2,29184]{1,0:T(2,128)S(1)} %copy-done.2), kind=kLoop, calls=%fused_computation.3 | loop fusion | flops 875520 | bytes 1634304 | tf_op jit(solution)/shard_map/sub | solution.py:725
  (1 shorter events, 0.0 us)
Async XLA Ops:
  2.3 0.9 copy-start.6
  2.4 1.6 %copy-start.3 = (bf16[13,25,256]{2,0,1:T(8,128)(2,1)S(1)}, bf16[13,25,256]{2,0,1:T(8,128)(2,1)}, u32[]{:S(2)}) copy-start(bf16[13,25,256]{2,0,1:T(8,128)(2,1)} %param.12) | copy-start | bytes 499204
  4.1 0.9 copy-start.4
  5.0 1.2 copy-start.5
  7.4 115.4 %copy-start.2 = (f32[2,29184]{1,0:T(2,128)S(1)}, f32[2,29184]{1,0:T(2,128)}, u32[]{:S(2)}) copy-start(f32[2,29184]{1,0:T(2,128)} %param.19) | copy-start | bytes 700420
  121.7 1.2 copy-start
  121.7 1.2 copy-start.1
